TPU v7x, 32 devices: a whole 2x2x4 slice. The times are simulated.
32 devices in a mesh: sec: 4 (over z), tile: 4 (over y, core), role: 2 (over x).
Axes of the slice: x: 2, y: 2, z: 4, core: 2. Of those that a mesh axis runs over, the one named last changes fastest.
Arguments:
- pressure: float32 [32, 256, 8192], P(None, 'sec', ('tile', 'role')), may hold values from -6 to 6
- cell_weight: float32 [8192], P(('tile', 'role')), may hold values from 0.25 to 4
- live_cells: int32 [8], replicated, may hold values from 341 to 1024, as said below
- mode_order: int32 [128], replicated, may hold values from 0 to 127, each once
Outputs:
- gram: float32 [128, 32, 32], P('sec', ('tile', 'role'))
Inputs may be any that keep to these rules, and one draw needn't show every extreme that they name: `live_cells`: at least one tile half is full. `mode_order`: each wavenumber appears once.
All inputs are finite; a program needn't handle non-finite values.
Results may differ from a plain program's by a relative error of at most 0.0003.
Values sent between devices are 32-bit elements; how exact they have to be, the bound alone decides.
A program may use at most 128 MiB of HBM per device.

v0:
```python
import math
import jax
import jax.numpy as jnp
from jax import lax
from jax.sharding import PartitionSpec as P


def time_table(count):
    steps = jnp.arange(count, dtype=jnp.int32)
    half = count // 2
    freqs = jnp.arange(half, dtype=jnp.int32)
    hann = 0.5 - 0.5 * jnp.cos(2.0 * math.pi * steps.astype(jnp.float32) / count)
    phase = 2.0 * math.pi * (freqs[:, None] * steps[None, :] % count).astype(jnp.float32) / count
    factor = math.sqrt(8.0 / (3.0 * count))
    return jnp.concatenate(
        [factor * hann[None, :] * jnp.cos(phase), -factor * hann[None, :] * jnp.sin(phase)], axis=0
    )


def angle_table(mode_order, angles):
    index = jnp.arange(angles, dtype=jnp.int32)
    phase = (
        2.0 * math.pi * (mode_order[:, None] * index[None, :] % angles).astype(jnp.float32) / angles
    )
    cosine = jnp.cos(phase) / math.sqrt(angles)
    sine = jnp.sin(phase) / math.sqrt(angles)
    return jnp.stack(
        [jnp.stack([cosine, sine], axis=1), jnp.stack([-sine, cosine], axis=1)], axis=0
    )


def on_device(pressure, cell_weight, live_cells, mode_order):
    hi = lax.Precision.HIGHEST
    snaps = pressure.shape[0]
    half = snaps // 2
    n_sec = lax.axis_size("sec")
    n_grp = lax.axis_size("tile") * lax.axis_size("role")
    angles = pressure.shape[1] * n_sec
    group_cells = pressure.shape[2]
    cell_dev = group_cells // n_sec
    modes = mode_order.shape[0]
    total_cells = group_cells * n_grp
    htab = time_table(snaps)
    atab = angle_table(mode_order, angles)
    arrived = lax.all_to_all(pressure, "sec", split_axis=2, concat_axis=1, tiled=True)
    spectra = jnp.einsum("rt,tqc->rqc", htab, arrived, precision=hi)
    split = spectra.reshape(2, half, angles, cell_dev)
    modal = jnp.einsum("okiq,ifqc->kofc", atab, split, precision=hi).reshape(modes, snaps, cell_dev)
    group = lax.axis_index("tile") * lax.axis_size("role") + lax.axis_index("role")
    live = lax.dynamic_slice_in_dim(live_cells, group, 1, 0)[0]
    owned = lax.all_to_all(modal, "sec", split_axis=0, concat_axis=2, tiled=True)
    position = jnp.arange(group_cells, dtype=jnp.int32)
    weighted = jnp.where(position < live, cell_weight / total_cells, jnp.float32(0.0))
    local_gram = jnp.einsum("kac,kbc->kab", owned * weighted[None, None, :], owned, precision=hi)
    result = lax.psum_scatter(local_gram, ("tile", "role"), scatter_dimension=1, tiled=True)
    return result


def solution(mesh):
    in_specs = (P(None, "sec", ("tile", "role")), P(("tile", "role")), P(), P())
    out_specs = P("sec", ("tile", "role"), None)
    return jax.shard_map(
        on_device, mesh=mesh, in_specs=in_specs, out_specs=out_specs, check_vma=False
    )
```

profile of v0, /device:TPU:0, one launch (start us, length us, event | category | flops | bytes accessed | tf_op | source)
XLA Modules:
  0.0 474.0 jit_solution(6145706416273522948)
XLA Ops:
  6.5 16.2 %copy.12 = f32[32,64,1024]{1,0,2:T(8,128)} copy(f32[32,64,1024]{2,1,0:T(8,128)} %param.4) | data formatting | bytes 16777216 | tf_op args[0]
  22.7 14.4 %reshape.145 = f32[4,1,524288]{2,1,0:T(1,128)} reshape(f32[1024,32,64]{2,1,0:T(8,128)} %bitcast.38) | data formatting | bytes 16777216
  37.1 0.0 copy-start.1
  37.1 6.5 %all-to-all-start = ((f32[4,1,524288]{2,1,0:T(1,128)}), f32[4,1,524288]{2,1,0:T(1,128)}, u32[]{:S(2)}, u32[]{:S(2)}) async-start(f32[4,1,524288]{2,1,0:T(1,128)} %reshape.145), calls=%async_computation | async-start | bytes 16777216 | tf_op jit(solution)/shard_map/all_to_all | solution.py:45
  43.7 0.1 sine_multiply_fusion.1
  43.8 0.0 copy-done.1
  43.8 0.6 sine_multiply_fusion
  44.4 183.2 %all-to-all-done = f32[4,1,524288]{2,1,0:T(1,128)} async-done(((f32[4,1,524288]{2,1,0:T(1,128)}), f32[4,1,524288]{2,1,0:T(1,128)}, u32[]{:S(2)}, u32[]{:S(2)}) %all-to-all-start) | async-done | bytes 8388640 | tf_op jit(solution)/shard_map/all_to_all | solution.py:45
  227.7 0.5 broadcast.237
  228.2 28.8 %reduce = f32[4,524288]{1,0:T(4,128)} reduce(f32[4,1,524288]{2,1,0:T(1,128)} %all-to-all-done, f32[]{:T(128)} %broadcast.237), dimensions={1}, to_apply=%all_to_all.26.reduce_sub_computation | reduce | bytes 16777220 | tf_op jit(solution)/shard_map/all_to_all | solution.py:45
  256.9 16.8 %reshape.146 = f32[1024,32,64]{2,1,0:T(8,128)} reshape(f32[4,524288]{1,0:T(4,128)} %reduce) | data formatting | bytes 16777216
  273.7 13.2 %copy.24 = f32[32,64,4,256]{3,2,1,0:T(4,128)} copy(f32[32,64,4,256]{1,0,3,2:T(8,128)} %bitcast.37) | data formatting | bytes 16777216 | tf_op jit(solution)/shard_map/all_to_all | solution.py:45
  286.9 8.2 %copy.25 = f32[32,4,64,256]{3,0,2,1:T(8,128)S(1)} copy(f32[32,4,64,256]{3,1,2,0:T(4,128)} %bitcast.40) | data formatting | bytes 16777216 | tf_op jit(solution)/shard_map/all_to_all | solution.py:45
  295.1 8.4 %convolution_bitcast_fusion = f32[2,16,256,256,1]{3,1,2,0,4:T(8,128)S(1)} fusion(f32[2,16,32,1]{2,1,3,0:T(8,128)S(1)} %bitcast.43, f32[32,256,256,1]{2,0,1,3:T(8,128)S(1)} %bitcast.41), kind=kOutput, calls=%fused_computation.4 | convolution fusion | flops 805306368 | bytes 16781312 | tf_op jit(solution)/shard_map/rt,tqc->rqc/dot_general | solution.py:46
  303.5 17.4 %fusion.4 = f32[128,2,16,256]{0,3,1,2:T(8,128)} fusion(f32[2,16,256,256,1]{3,1,2,0,4:T(8,128)S(1)} %convolution_bitcast_fusion, f32[1,128,2,256]{3,1,2,0:T(8,128)S(1)} %get-tuple-element.6, f32[1,128,2,256]{3,1,2,0:T(8,128)S(1)} %get-tuple-element.5), kind=kOutput, calls=%fused_computation.5 | convolution fusion | flops 6442582016 | bytes 13107200 | tf_op jit(solution)/shard_map/okiq,ifqc->kofc/dot_general | solution.py:48
  320.9 0.0 copy-start.2
  320.9 0.0 copy-start
  320.9 5.5 %copy.17 = f32[128,2,16,256]{3,2,1,0:T(8,128)} copy(f32[128,2,16,256]{0,3,1,2:T(8,128)} %fusion.4) | data formatting | bytes 8388608 | tf_op jit(solution)/shard_map/okiq,ifqc->kofc/transpose | solution.py:48
  326.5 4.8 %all-to-all-start.1 = ((f32[128,32,256]{2,1,0:T(8,128)}), f32[128,32,256]{2,1,0:T(8,128)}, u32[]{:S(2)}, u32[]{:S(2)}) async-start(f32[128,32,256]{2,1,0:T(8,128)} %bitcast.42), calls=%async_computation.1 | async-start | bytes 8388608 | tf_op jit(solution)/shard_map/all_to_all | solution.py:51
  331.3 0.3 reduce-scatter.2.cloned.1.call-start
  331.6 0.0 copy-done.2
  331.7 0.6 dynamic_slice.3
  332.2 0.0 copy-done
  332.2 0.6 multiply_select_fusion
  332.9 91.3 %all-to-all-done.1 = f32[128,32,256]{2,1,0:T(8,128)} async-done(((f32[128,32,256]{2,1,0:T(8,128)}), f32[128,32,256]{2,1,0:T(8,128)}, u32[]{:S(2)}, u32[]{:S(2)}) %all-to-all-start.1) | async-done | bytes 4194336 | tf_op jit(solution)/shard_map/all_to_all | solution.py:51
  424.2 2.7 copy.28
  426.9 4.1 fusion.2
  431.0 1.1 copy.19
  432.1 0.0 reduce-scatter.2.cloned.1.call-update
  432.1 33.2 %reduce-scatter.2.cloned.1.call-done = f32[32,4,32]{2,0,1:T(8,128)} async-done(((f32[32,32,32]{2,0,1:T(8,128)}), f32[32,4,32]{2,0,1:T(8,128)}) %reduce-scatter.2.cloned.1.call-update) | async-done | bytes 16400 | tf_op jit(solution)/shard_map/reduce_scatter | solution.py:55
  465.4 1.5 copy.20
  (4 shorter events, 0.1 us)
Async XLA Ops:
  37.1 6.7 %copy-start.1 = (s32[128]{0:T(128)S(1)}, s32[128]{0:T(128)}, u32[]{:S(2)}) copy-start(s32[128]{0:T(128)} %param.7) | copy-start | bytes 1540
  37.1 190.6 %all-to-all-start = ((f32[4,1,524288]{2,1,0:T(1,128)}), f32[4,1,524288]{2,1,0:T(1,128)}, u32[]{:S(2)}, u32[]{:S(2)}) async-start(f32[4,1,524288]{2,1,0:T(1,128)} %reshape.145), calls=%async_computation | async-start | bytes 16777216 | tf_op jit(solution)/shard_map/all_to_all | solution.py:45
  320.9 10.7 %copy-start.2 = (s32[8]{0:T(128)S(1)}, s32[8]{0:T(128)}, u32[]{:S(2)}) copy-start(s32[8]{0:T(128)} %param.6) | copy-start | bytes 100
  320.9 11.3 %copy-start = (f32[1024]{0:T(1024)S(1)}, f32[1024]{0:T(1024)}, u32[]{:S(2)}) copy-start(f32[1024]{0:T(1024)} %param.5) | copy-start | bytes 12292
  326.5 97.7 %all-to-all-start.1 = ((f32[128,32,256]{2,1,0:T(8,128)}), f32[128,32,256]{2,1,0:T(8,128)}, u32[]{:S(2)}, u32[]{:S(2)}) async-start(f32[128,32,256]{2,1,0:T(8,128)} %bitcast.42), calls=%async_computation.1 | async-start | bytes 8388608 | tf_op jit(solution)/shard_map/all_to_all | solution.py:51
  331.3 134.0 %reduce-scatter.2.cloned.1.call-start = ((), (), s32[]{:S(2)}) async-start(), calls=%async_computation.3 | async-start | bytes 589824 | tf_op jit(solution)/shard_map/reduce_scatter | solution.py:55
Sparse Core Ops, SparseCore 0:
  432.3 33.0 reduce-scatter.1
where the time goes:
time: 480 us; the launch traced here: 474 us
  waiting for transfers between devices  308 us (64%)
  local copies, waits for them, and re-layouts  80.7 us (17%)
  other arithmetic  30.2 us (6%)
  matrix products  29.9 us (6%)
  between operations  13.8 us (3%)
  starting transfers between devices  11.6 us (2%)
    all_to_all x1, waiting for transfers between devices, on_device(): lax.all_to_all(pressure, 'sec', split_axis=2, concat_axis=1, tiled=True)  183 us
    all_to_all x1, waiting for transfers between devices, on_device(): lax.all_to_all(modal, 'sec', split_axis=0, concat_axis=2, tiled=True)  91.3 us
    unnamed x9, local copies, waits for them, and re-layouts  47.3 us
    reduce_scatter x1, waiting for transfers between devices, on_device(): lax.psum_scatter(local_gram, ('tile', 'role'), scatter_dimension=1, tiled...  33.2 us
    all_to_all x1, other arithmetic, on_device(): lax.all_to_all(pressure, 'sec', split_axis=2, concat_axis=1, tiled=True)  28.8 us
    all_to_all x3, local copies, waits for them, and re-layouts, on_device(): lax.all_to_all(pressure, 'sec', split_axis=2, concat_axis=1, tiled=True)  21.9 us
    dot_general x1, matrix products, on_device(): jnp.einsum('okiq,ifqc->kofc', atab, split, precision=hi)  17.4 us
  transfers between devices with their start and end apart: 3, of which 3 were waited for; matrix products, arithmetic and copies ran while one was open for 0% of the time, Pallas kernels for 0%

commit v1 on v0

--- a/solution.py
+++ b/solution.py
@@ -42,7 +42,15 @@
     total_cells = group_cells * n_grp
     htab = time_table(snaps)
     atab = angle_table(mode_order, angles)
-    arrived = lax.all_to_all(pressure, "sec", split_axis=2, concat_axis=1, tiled=True)
+    arrived = jnp.concatenate(
+        lax.all_to_all(
+            jnp.stack(jnp.split(pressure, lax.axis_size("sec"), axis=2), axis=0),
+            axis_name="sec",
+            split_axis=0,
+            concat_axis=0,
+        ),
+        1,
+    )
     spectra = jnp.einsum("rt,tqc->rqc", htab, arrived, precision=hi)
     split = spectra.reshape(2, half, angles, cell_dev)
     modal = jnp.einsum("okiq,ifqc->kofc", atab, split, precision=hi).reshape(modes, snaps, cell_dev)

time: 480 us -> 392 us (0.82); the launches traced: 474 us -> 392 us
  local copies, waits for them, and re-layouts: 80.7 us -> 19.5 us
  other arithmetic: 30.2 us -> 4.98 us
    unnamed x9 -> x6, local copies, waits for them, and re-layouts: 47.3 us -> 0.01 us
    all_to_all x1 -> x0, other arithmetic: 28.8 us -> none  [on_device(): lax.all_to_all(pressure, 'sec', split_axis=2, concat_axis=1, tiled=True)]
    all_to_all x3 -> x1, local copies, waits for them, and re-layouts: 21.9 us -> 3.99 us  [on_device(): lax.all_to_all(jnp.stack(jnp.split(pressure, lax.axis_size('sec'), axis=2...]
  transfers between devices with their start and end apart: 3 -> 3, of which waited for: 3 -> 3; matrix products, arithmetic and copies ran while one was open for 0% -> 1% of each run, Pallas kernels for 0% -> 0%
where the time goes in v1:
time: 392 us
  waiting for transfers between devices  308 us (79%)
  matrix products  34.2 us (9%)
  local copies, waits for them, and re-layouts  19.5 us (5%)
  between operations  13.5 us (3%)
  starting transfers between devices  11.7 us (3%)
  other arithmetic  4.98 us (1%)
    all_to_all x1, waiting for transfers between devices, on_device(): lax.all_to_all(jnp.stack(jnp.split(pressure, lax.axis_size('sec'), axis=2...  183 us
    all_to_all x1, waiting for transfers between devices, on_device(): lax.all_to_all(modal, 'sec', split_axis=0, concat_axis=2, tiled=True)  91.4 us
    reduce_scatter x1, waiting for transfers between devices, on_device(): lax.psum_scatter(local_gram, ('tile', 'role'), scatter_dimension=1, tiled...  33.2 us
    dot_general x1, matrix products, on_device(): jnp.einsum('okiq,ifqc->kofc', atab, split, precision=hi)  17.3 us
    dot_general x1, matrix products, on_device(): spectra = jnp.einsum('rt,tqc->rqc', htab, arrived, precision=hi)  12.8 us
  transfers between devices with their start and end apart: 3, of which 3 were waited for; matrix products, arithmetic and copies ran while one was open for 1% of the time, Pallas kernels for 0%

profile of v1, /device:TPU:0, one launch (start us, length us, event | category | flops | bytes accessed | tf_op | source)
XLA Modules:
  0.0 391.8 jit_solution(8651425654973589464)
XLA Ops:
  6.5 4.1 %slice_bitcast_fusion.3 = (f32[1,32,64,256]{3,2,1,0:T(8,128)S(1)}, f32[1,32,64,256]{3,2,1,0:T(8,128)S(1)}, f32[1,32,64,256]{3,2,1,0:T(8,128)S(1)}, f32[1,32,64,256]{3,2,1,0:T(8,128)S(1)}) fusion(f32[32,64,1024]{2,1,0:T(8,128)} %param.4), kind=kLoop, calls=%fused_computation.14 | loop fusion | bytes 16777216 | tf_op jit(solution)/shard_map/stack | solution.py:47
  10.7 3.5 pad_maximum_fusion
  14.2 0.0 copy-start.1
  14.2 6.5 %all-to-all-start = ((f32[4,32,64,256]{3,2,1,0:T(8,128)}), f32[4,32,64,256]{3,2,1,0:T(8,128)}, u32[]{:S(2)}, u32[]{:S(2)}) async-start(f32[4,32,64,256]{3,2,1,0:T(8,128)} %pad_maximum_fusion), calls=%async_computation | async-start | bytes 16777216 | tf_op jit(solution)/shard_map/all_to_all | solution.py:46
  20.8 0.1 sine_multiply_fusion.1
  20.9 0.0 copy-done.1
  20.9 0.6 sine_multiply_fusion
  21.5 183.2 %all-to-all-done = f32[4,32,64,256]{3,2,1,0:T(8,128)} async-done(((f32[4,32,64,256]{3,2,1,0:T(8,128)}), f32[4,32,64,256]{3,2,1,0:T(8,128)}, u32[]{:S(2)}, u32[]{:S(2)}) %all-to-all-start) | async-done | bytes 8388640 | tf_op jit(solution)/shard_map/all_to_all | solution.py:46
  204.8 4.0 %copy.7 = f32[4,32,64,256]{3,2,0,1:T(8,128)S(1)} copy(f32[4,32,64,256]{3,2,1,0:T(8,128)} %all-to-all-done) | data formatting | bytes 16777216 | tf_op jit(solution)/shard_map/all_to_all | solution.py:46
  208.8 12.8 %fusion.7 = f32[2,16,256,256,1]{3,1,2,0,4:T(8,128)S(1)} fusion(f32[2,16,32,1]{2,1,3,0:T(8,128)S(1)} %bitcast.47, f32[32,256,256]{2,1,0:T(8,128)S(1)} %bitcast.45), kind=kOutput, calls=%fused_computation.8 | convolution fusion | flops 805306368 | bytes 16781312 | tf_op jit(solution)/shard_map/rt,tqc->rqc/dot_general | solution.py:54
  221.6 17.3 %fusion.10 = f32[128,2,16,256]{0,3,1,2:T(8,128)} fusion(f32[2,16,256,256,1]{3,1,2,0,4:T(8,128)S(1)} %fusion.7, f32[1,128,2,256]{3,1,2,0:T(8,128)S(1)} %get-tuple-element.10, f32[1,128,2,256]{3,1,2,0:T(8,128)S(1)} %get-tuple-element.9), kind=kOutput, calls=%fused_computation.9 | convolution fusion | flops 6442582016 | bytes 13107200 | tf_op jit(solution)/shard_map/okiq,ifqc->kofc/dot_general | solution.py:56
  238.9 5.5 %copy.10 = f32[128,2,16,256]{3,2,1,0:T(8,128)} copy(f32[128,2,16,256]{0,3,1,2:T(8,128)} %fusion.10) | data formatting | bytes 8388608 | tf_op jit(solution)/shard_map/okiq,ifqc->kofc/transpose | solution.py:56
  244.4 0.0 copy-start.2
  244.4 0.0 copy-start
  244.4 5.0 %all-to-all-start.1 = ((f32[128,32,256]{2,1,0:T(8,128)}), f32[128,32,256]{2,1,0:T(8,128)}, u32[]{:S(2)}, u32[]{:S(2)}) async-start(f32[128,32,256]{2,1,0:T(8,128)} %bitcast.46), calls=%async_computation.1 | async-start | bytes 8388608 | tf_op jit(solution)/shard_map/all_to_all | solution.py:59
  249.4 0.3 reduce-scatter.2.cloned.1.call-start
  249.7 0.0 copy-done.2
  249.7 0.6 dynamic_slice.3
  250.3 0.0 copy-done
  250.3 0.6 multiply_select_fusion
  250.9 91.4 %all-to-all-done.1 = f32[128,32,256]{2,1,0:T(8,128)} async-done(((f32[128,32,256]{2,1,0:T(8,128)}), f32[128,32,256]{2,1,0:T(8,128)}, u32[]{:S(2)}, u32[]{:S(2)}) %all-to-all-start.1) | async-done | bytes 4194336 | tf_op jit(solution)/shard_map/all_to_all | solution.py:59
  342.3 2.7 copy.19
  345.0 4.1 %fusion.5 = f32[32,32,32]{2,1,0:T(8,128)S(1)} fusion(f32[32,32,1024]{2,1,0:T(8,128)S(1)} %bitcast.44, f32[1024]{0:T(1024)S(1)} %multiply_select_fusion), kind=kOutput, calls=%fused_computation.6 | convolution fusion | flops 403701760 | bytes 4329472 | tf_op jit(solution)/shard_map/kac,kbc->kab/dot_general | solution.py:62
  349.1 1.1 copy.12
  350.2 0.0 reduce-scatter.2.cloned.1.call-update
  350.2 33.2 %reduce-scatter.2.cloned.1.call-done = f32[32,4,32]{2,0,1:T(8,128)} async-done(((f32[32,32,32]{2,0,1:T(8,128)}), f32[32,4,32]{2,0,1:T(8,128)}) %reduce-scatter.2.cloned.1.call-update) | async-done | bytes 16400 | tf_op jit(solution)/shard_map/reduce_scatter | solution.py:63
  383.4 1.5 copy.13
  (4 shorter events, 0.1 us)
Async XLA Ops:
  14.2 6.7 %copy-start.1 = (s32[128]{0:T(128)S(1)}, s32[128]{0:T(128)}, u32[]{:S(2)}) copy-start(s32[128]{0:T(128)} %param.7) | copy-start | bytes 1540
  14.2 190.6 %all-to-all-start = ((f32[4,32,64,256]{3,2,1,0:T(8,128)}), f32[4,32,64,256]{3,2,1,0:T(8,128)}, u32[]{:S(2)}, u32[]{:S(2)}) async-start(f32[4,32,64,256]{3,2,1,0:T(8,128)} %pad_maximum_fusion), calls=%async_computation | async-start | bytes 16777216 | tf_op jit(solution)/shard_map/all_to_all | solution.py:46
  244.4 5.3 %copy-start.2 = (s32[8]{0:T(128)S(1)}, s32[8]{0:T(128)}, u32[]{:S(2)}) copy-start(s32[8]{0:T(128)} %param.6) | copy-start | bytes 100
  244.4 5.9 %copy-start = (f32[1024]{0:T(1024)S(1)}, f32[1024]{0:T(1024)}, u32[]{:S(2)}) copy-start(f32[1024]{0:T(1024)} %param.5) | copy-start | bytes 12292
  244.4 97.9 %all-to-all-start.1 = ((f32[128,32,256]{2,1,0:T(8,128)}), f32[128,32,256]{2,1,0:T(8,128)}, u32[]{:S(2)}, u32[]{:S(2)}) async-start(f32[128,32,256]{2,1,0:T(8,128)} %bitcast.46), calls=%async_computation.1 | async-start | bytes 8388608 | tf_op jit(solution)/shard_map/all_to_all | solution.py:59
  249.4 134.0 %reduce-scatter.2.cloned.1.call-start = ((), (), s32[]{:S(2)}) async-start(), calls=%async_computation.3 | async-start | bytes 589824 | tf_op jit(solution)/shard_map/reduce_scatter | solution.py:63
Sparse Core Ops, SparseCore 0:
  350.3 33.0 reduce-scatter.1
